TPU v7x, 32 devices: a whole 2x2x4 slice. The times are simulated.
32 devices in a mesh: ha: 2 (over y), wa: 16 (over z, x, core).
Axes of the slice: x: 2, y: 2, z: 4, core: 2. Of those that a mesh axis runs over, the one named last changes fastest.
Arguments:
- block_input: bfloat16 [3, 46, 160, 128], P(None, 'ha', 'wa'), may hold values from -6 to 6
- cotangent: bfloat16 [3, 46, 160, 128], P(None, 'ha', 'wa'), may hold values from -6 to 6
- kernel_one: bfloat16 [3, 3, 3, 128, 128], replicated, may hold values from -0.109375 to 0.109375
- bias_one: float32 [128], replicated, may hold values from -3 to 3
- kernel_two: bfloat16 [3, 3, 3, 128, 128], replicated, may hold values from -0.109375 to 0.109375
- scale_one: float32 [128], replicated, may hold values from 0.5 to 2
- shift_one: float32 [128], replicated, may hold values from -1 to 1
- scale_two: float32 [128], replicated, may hold values from 0.5 to 2
- shift_two: float32 [128], replicated, may hold values from -1 to 1
Outputs:
- grad_input: bfloat16 [3, 46, 160, 128], P(None, 'ha', 'wa')
- grad_kernel_one: float32 [3, 3, 3, 128, 128], replicated
- grad_bias_one: float32 [128], replicated
- grad_kernel_two: float32 [3, 3, 3, 128, 128], replicated
- grad_bias_two: float32 [128], replicated
All inputs are finite; a program needn't handle non-finite values.
Results may differ from a plain program's by a relative error of at most 0.0054.
Values may be sent and summed in bfloat16 or wider, within the bound.
A program may use at most 64 MiB of HBM per device.

v0:
```python
import math
import jax
import jax.numpy as jnp
from jax import lax
from jax.sharding import PartitionSpec as P


def with_halo(cells, sides, width):
    for axis, dim in sides:
        count = lax.axis_size(axis)
        ends = count - 1
        head = lax.slice_in_dim(cells, 0, width, axis=dim)
        tail = lax.slice_in_dim(cells, cells.shape[dim] - width, cells.shape[dim], axis=dim)
        cells = jnp.concatenate(
            [
                lax.ppermute(tail, axis, [(i, (i + 1) % count) for i in range(ends)]),
                cells,
                lax.ppermute(head, axis, [((i + 1) % count, i) for i in range(ends)]),
            ],
            axis=dim,
        )
    return cells


def slope(value):
    sigma = jax.nn.sigmoid(value)
    return sigma * (1.0 + value * (1.0 - sigma))


def widen(padded, columns):
    return jnp.concatenate([padded[:, :, shift : shift + columns] for shift in range(3)], axis=-1)


def convolve(wide, kernel, frames, rows):
    columns = wide.shape[2]
    inner = kernel.shape[3]
    total = jnp.zeros((frames * rows * columns, kernel.shape[4]), jnp.float32)
    for step_t in range(3):
        for step_h in range(3):
            slab = wide[step_t : step_t + frames, step_h : step_h + rows].reshape(-1, 3 * inner)
            total = total + jnp.dot(
                slab,
                kernel[step_t, step_h].reshape(3 * inner, -1),
                preferred_element_type=jnp.float32,
            )
    return total.reshape(frames, rows, columns, -1)


def kernel_terms(wide, grads, frames, rows):
    inner = wide.shape[3] // 3
    pieces = []
    for step_t in range(3):
        for step_h in range(3):
            slab = wide[step_t : step_t + frames, step_h : step_h + rows].reshape(-1, 3 * inner)
            pieces.append(
                lax.dot_general(
                    slab, grads, (((0,), (0,)), ((), ())), preferred_element_type=jnp.float32
                )
            )
    return jnp.stack(pieces).reshape(3, 3, 3, inner, grads.shape[1])


def flipped(kernel):
    return jnp.transpose(kernel[::-1, ::-1, ::-1], (0, 1, 2, 4, 3))


def body(
    block_input,
    cotangent,
    kernel_one,
    bias_one,
    kernel_two,
    scale_one,
    shift_one,
    scale_two,
    shift_two,
):
    frames, rows, columns, chans = block_input.shape
    factor = 1.0 / math.sqrt(frames * rows * lax.axis_size("ha") * columns * lax.axis_size("wa"))
    front = ((2, 0), (0, 0), (0, 0), (0, 0))
    back = ((0, 2), (0, 0), (0, 0), (0, 0))
    first_pre = block_input.astype(jnp.float32) * scale_one + shift_one
    first_act = jax.nn.silu(first_pre).astype(jnp.bfloat16)
    joined = with_halo(jnp.stack([first_act, cotangent]), (("ha", 2), ("wa", 3)), 1)
    first_rim = joined[0]
    cot_halo = joined[1]
    first_wide = widen(jnp.pad(first_rim, front), columns)
    hidden = convolve(first_wide, kernel_one, frames, rows) + bias_one
    second_pre = hidden * scale_two + shift_two
    second_act = jax.nn.silu(second_pre).astype(jnp.bfloat16)
    second_rim = with_halo(second_act, (("ha", 1), ("wa", 2)), 1)
    second_wide = widen(jnp.pad(second_rim, front), columns)
    upstream = cotangent.reshape(-1, chans)
    grad_two = kernel_terms(second_wide, upstream, frames, rows)
    bias_b = jnp.sum(cotangent.astype(jnp.float32), axis=(0, 1, 2))
    cot_wide = widen(jnp.pad(cot_halo, back), columns)
    back_two = convolve(cot_wide, flipped(kernel_two), frames, rows)
    inner = (back_two * slope(second_pre) * scale_two).astype(jnp.bfloat16)
    inner_rim = with_halo(inner, (("ha", 1), ("wa", 2)), 1)
    inner_wide = widen(jnp.pad(inner_rim, back), columns)
    back_one = convolve(inner_wide, flipped(kernel_one), frames, rows)
    grad_input = (cotangent.astype(jnp.float32) + back_one * slope(first_pre) * scale_one).astype(
        jnp.bfloat16
    )
    grad_one = kernel_terms(first_wide, inner.reshape(-1, chans), frames, rows)
    bias_a = jnp.sum(inner.astype(jnp.float32), axis=(0, 1, 2))
    grad_one, bias_a, grad_two, bias_b = lax.psum(
        (grad_one, bias_a, grad_two, bias_b), ("ha", "wa")
    )
    return (grad_input, grad_one * factor, bias_a * factor, grad_two * factor, bias_b * factor)


def solution(mesh):
    return jax.shard_map(
        body,
        mesh=mesh,
        in_specs=(
            P(None, "ha", "wa", None),
            P(None, "ha", "wa", None),
            P(),
            P(),
            P(),
            P(),
            P(),
            P(),
            P(),
        ),
        out_specs=(P(None, "ha", "wa", None), P(), P(), P(), P()),
        check_vma=False,
    )
```

profile of v0, /device:TPU:0, one launch (start us, length us, event | category | flops | bytes accessed | tf_op | source)
XLA Modules:
  0.0 281.3 jit_solution(7883911846606421409)
XLA Ops:
  7.2 1.1 fusion.51
  9.3 4.9 %collective-permute-start = (bf16[2,3,1,10,128]{4,2,3,1,0:T(2,128)(2,1)S(1)}, bf16[2,3,1,10,128]{4,2,3,1,0:T(2,128)(2,1)S(1)}, u32[]{:S(2)}, u32[]{:S(2)}) collective-permute-start(bf16[2,3,1,10,128]{4,2,3,1,0:T(2,128)(2,1)S(1)} %get-tuple-element.75), channel_id=1, source_target_pairs={{0,16},{1,17},{2,18},{3,19},{4,20},{5,21},{6,22},{7,23},{8,24},{9,... | collective-permute-start | bytes 46088 | tf_op jit(solution)/shard_map/ppermute | solution.py:16
  14.2 1.3 collective-permute-start.1
  15.5 2.2 fusion.65
  17.7 1.4 copy.39
  19.0 2.0 copy.18
  22.3 1.5 collective-permute-start.2
  23.7 1.3 collective-permute-start.3
  26.0 2.5 collective-permute-done.3
  28.7 1.3 pad_slice_fusion.2
  30.2 1.9 fusion.63
  33.3 1.2 copy.19
  35.4 1.2 copy.20
  37.6 1.2 copy.21
  39.8 1.2 copy.22
  45.3 1.4 pad_maximum_fusion.1
  46.6 2.3 fusion.62
  50.1 1.2 copy.28
  52.3 1.2 copy.29
  54.5 1.2 copy.30
  56.6 1.2 copy.31
  58.8 1.2 copy.32
  61.0 1.2 copy.33
  63.1 1.2 copy.34
  67.6 1.3 fusion.72
  69.0 1.3 convolution_add_fusion.15
  73.3 1.3 fusion.71
  74.6 1.5 convolution_add_fusion.23
  79.6 4.5 %collective-permute-start.4 = (bf16[3,1,10,128]{3,1,2,0:T(2,128)(2,1)S(1)}, bf16[3,1,10,128]{3,1,2,0:T(2,128)(2,1)S(1)}, u32[]{:S(2)}, u32[]{:S(2)}) collective-permute-start(bf16[3,1,10,128]{3,1,2,0:T(2,128)(2,1)S(1)} %get-tuple-element.91), channel_id=1, source_target_pairs={{0,16},{1,17},{2,18},{3,19},{4,20},{5,21},{6,22},{7,23},{8,24},{9,... | collective-permute-start | bytes 23048 | tf_op jit(solution)/shard_map/ppermute | solution.py:16
  84.1 1.3 collective-permute-start.5
  85.5 4.5 %collective-permute-start.8 = (bf16[3,1,10,128]{3,1,2,0:T(2,128)(2,1)S(1)}, bf16[3,1,10,128]{3,1,2,0:T(2,128)(2,1)S(1)}, u32[]{:S(2)}, u32[]{:S(2)}) collective-permute-start(bf16[3,1,10,128]{3,1,2,0:T(2,128)(2,1)S(1)} %get-tuple-element.89), channel_id=1, source_target_pairs={{0,16},{1,17},{2,18},{3,19},{4,20},{5,21},{6,22},{7,23},{8,24},{9,... | collective-permute-start | bytes 23048 | tf_op jit(solution)/shard_map/ppermute | solution.py:16
  90.0 1.3 collective-permute-start.9
  94.3 3.9 %collective-permute-start.6 = (bf16[3,25,1,128]{3,1,2,0:T(8,128)(2,1)S(1)}, bf16[3,25,1,128]{3,1,2,0:T(8,128)(2,1)S(1)}, u32[]{:S(2)}, u32[]{:S(2)}) collective-permute-start(bf16[3,25,1,128]{3,1,2,0:T(8,128)(2,1)S(1)} %get-tuple-element.85), channel_id=1, source_target_pairs={{0,1},{1,2},{2,3},{3,4},{4,5},{5,6},{6,7},{7,8},{8,9},{9,10},{10,1... | collective-permute-start | bytes 57608 | tf_op jit(solution)/shard_map/ppermute | solution.py:16
  98.2 1.3 collective-permute-start.7
  100.2 3.9 %collective-permute-start.10 = (bf16[3,25,1,128]{3,1,2,0:T(8,128)(2,1)}, bf16[3,25,1,128]{3,1,2,0:T(8,128)(2,1)}, u32[]{:S(2)}, u32[]{:S(2)}) collective-permute-start(bf16[3,25,1,128]{3,1,2,0:T(8,128)(2,1)} %get-tuple-element.83), channel_id=1, source_target_pairs={{0,1},{1,2},{2,3},{3,4},{4,5},{5,6},{6,7},{7,8},{8,9},{9,10},{10,1... | collective-permute-start | bytes 57608 | tf_op jit(solution)/shard_map/ppermute | solution.py:16
  104.1 1.3 collective-permute-start.11
  106.0 1.9 fusion.61
  109.0 1.2 copy.40
  111.2 1.2 copy.41
  113.4 1.2 copy.42
  115.5 1.2 copy.43
  125.2 1.4 convolution_add_fusion.7
  126.6 1.2 convolution_add_fusion.6
  132.3 1.4 convolution_add_fusion.3
  135.9 45.0 %all-reduce.4 = (f32[128]{0:T(128)S(1)}, f32[128]{0:T(128)S(1)}) all-reduce(f32[128]{0:T(128)S(1)} %get-tuple-element.93, f32[128]{0:T(128)S(1)} %get-tuple-element.87), channel_id=1, replica_groups=mesh['ha'=2,'wa'=16] {'ha','wa'}, use_global_device_ids=true, to_apply=%region_2.3 | all-reduce | flops 256 | bytes 2048 | tf_op jit(solution)/shard_map/psum | solution.py:107
  181.9 88.1 %all-reduce.8.cloned.1.call-done = (f32[3,3,3,128,128]{4,3,2,1,0:T(8,128)}, f32[3,3,3,128,128]{4,3,2,1,0:T(8,128)}) async-done(((f32[3,3,3,128,128]{4,3,2,1,0:T(8,128)}, f32[3,3,3,128,128]{4,3,2,1,0:T(8,128)}), (f32[3,3,3,128,128]{4,3,2,1,0:T(8,128)}, f32[3,3,3,128,128]{4,3,2,1,0:T(8,128)})) %all-reduce.8.cloned.1.call-update) | async-done | bytes 3538960 | tf_op jit(solution)/shard_map/psum | solution.py:107
  270.0 3.1 %broadcast_multiply_fusion = f32[3,3,3,128,128]{4,3,2,1,0:T(8,128)} fusion(f32[3,3,3,128,128]{4,3,2,1,0:T(8,128)} %get-tuple-element.8), kind=kLoop, calls=%fused_computation.76 | loop fusion | flops 442368 | bytes 3538944 | tf_op jit(solution)/shard_map/mul | solution.py:110
  273.1 1.4 broadcast_multiply_fusion.1
  (232 shorter events, 52.5 us)
Async XLA Ops:
  7.2 10.5 %copy-start = (bf16[3,3,3,128,128]{4,3,2,1,0:T(8,128)(2,1)S(1)}, bf16[3,3,3,128,128]{4,3,2,1,0:T(8,128)(2,1)}, u32[]{:S(2)}) copy-start(bf16[3,3,3,128,128]{4,3,2,1,0:T(8,128)(2,1)} %param.11) | copy-start | bytes 2654212
  7.2 262.8 %all-reduce.8.cloned.1.call-start = ((), (), s32[]{:S(2)}) async-start(), calls=%async_computation | async-start | bytes 7077888 | tf_op jit(solution)/shard_map/psum | solution.py:107
  9.3 12.9 %collective-permute-start = (bf16[2,3,1,10,128]{4,2,3,1,0:T(2,128)(2,1)S(1)}, bf16[2,3,1,10,128]{4,2,3,1,0:T(2,128)(2,1)S(1)}, u32[]{:S(2)}, u32[]{:S(2)}) collective-permute-start(bf16[2,3,1,10,128]{4,2,3,1,0:T(2,128)(2,1)S(1)} %get-tuple-element.75), channel_id=1, source_target_pairs={{0,16},{1,17},{2,18},{3,19},{4,20},{5,21},{6,22},{7,23},{8,24},{9,... | collective-permute-start | bytes 46088 | tf_op jit(solution)/shard_map/ppermute | solution.py:16
  14.2 8.0 %collective-permute-start.1 = (bf16[2,3,1,10,128]{4,2,3,1,0:T(2,128)(2,1)S(1)}, bf16[2,3,1,10,128]{4,2,3,1,0:T(2,128)(2,1)S(1)}, u32[]{:S(2)}, u32[]{:S(2)}) collective-permute-start(bf16[2,3,1,10,128]{4,2,3,1,0:T(2,128)(2,1)S(1)} %get-tuple-element.76), channel_id=1, source_target_pairs={{16,0},{17,1},{18,2},{19,3},{20,4},{21,5},{22,6},{23,7},{24,8},{25... | collective-permute-start | bytes 46088 | tf_op jit(solution)/shard_map/ppermute | solution.py:18
  22.3 3.7 %collective-permute-start.2 = (bf16[2,3,25,1,128]{4,2,3,1,0:T(8,128)(2,1)S(1)}, bf16[2,3,25,1,128]{4,2,3,1,0:T(8,128)(2,1)S(1)}, u32[]{:S(2)}, u32[]{:S(2)}) collective-permute-start(bf16[2,3,25,1,128]{4,2,3,1,0:T(8,128)(2,1)S(1)} %get-tuple-element.73), channel_id=1, source_target_pairs={{0,1},{1,2},{2,3},{3,4},{4,5},{5,6},{6,7},{7,8},{8,9},{9,10},{10,1... | collective-permute-start | bytes 115208 | tf_op jit(solution)/shard_map/ppermute | solution.py:16
  23.7 4.7 %collective-permute-start.3 = (bf16[2,3,25,1,128]{4,2,3,1,0:T(8,128)(2,1)S(1)}, bf16[2,3,25,1,128]{4,2,3,1,0:T(8,128)(2,1)S(1)}, u32[]{:S(2)}, u32[]{:S(2)}) collective-permute-start(bf16[2,3,25,1,128]{4,2,3,1,0:T(8,128)(2,1)S(1)} %get-tuple-element.74), channel_id=1, source_target_pairs={{1,0},{2,1},{3,2},{4,3},{5,4},{6,5},{7,6},{8,7},{9,8},{10,9},{11,1... | collective-permute-start | bytes 115208 | tf_op jit(solution)/shard_map/ppermute | solution.py:18
  43.2 2.1 copy-start.29
  66.6 2.4 copy-start.16
  67.6 2.7 copy-start.17
  67.6 2.7 copy-start.50
  67.6 3.1 %copy-start.18 = (bf16[690,384]{1,0:T(8,128)(2,1)S(1)}, bf16[690,384]{1,0:T(8,128)(2,1)}, u32[]{:S(2)}) copy-start(bf16[690,384]{1,0:T(8,128)(2,1)} %reshape.144) | copy-start | bytes 1589764
  67.6 3.1 %copy-start.49 = (bf16[1,1,3,128,128]{4,3,2,1,0:T(8,128)(2,1)S(1)}, bf16[1,1,3,128,128]{4,3,2,1,0:T(8,128)(2,1)}, u32[]{:S(2)}) copy-start(bf16[1,1,3,128,128]{4,3,2,1,0:T(8,128)(2,1)} %get-tuple-element.50) | copy-start | bytes 294916
  68.9 2.1 copy-start.19
  69.0 2.1 copy-start.48
  72.6 2.1 copy-start.3
  73.0 3.1 %copy-start.4 = (bf16[690,384]{1,0:T(8,128)(2,1)S(1)}, bf16[690,384]{1,0:T(8,128)(2,1)}, u32[]{:S(2)}) copy-start(bf16[690,384]{1,0:T(8,128)(2,1)} %reshape.133) | copy-start | bytes 1589764
  73.0 3.1 %copy-start.43 = (bf16[1,1,3,128,128]{4,3,2,1,0:T(8,128)(2,1)S(1)}, bf16[1,1,3,128,128]{4,3,2,1,0:T(8,128)(2,1)}, u32[]{:S(2)}) copy-start(bf16[1,1,3,128,128]{4,3,2,1,0:T(8,128)(2,1)} %get-tuple-element.60) | copy-start | bytes 294916
  73.3 3.2 %copy-start.5 = (bf16[690,384]{1,0:T(8,128)(2,1)S(1)}, bf16[690,384]{1,0:T(8,128)(2,1)}, u32[]{:S(2)}) copy-start(bf16[690,384]{1,0:T(8,128)(2,1)} %reshape.134) | copy-start | bytes 1589764
  73.3 3.2 %copy-start.42 = (bf16[1,1,3,128,128]{4,3,2,1,0:T(8,128)(2,1)S(1)}, bf16[1,1,3,128,128]{4,3,2,1,0:T(8,128)(2,1)}, u32[]{:S(2)}) copy-start(bf16[1,1,3,128,128]{4,3,2,1,0:T(8,128)(2,1)} %get-tuple-element.59) | copy-start | bytes 294916
  74.6 2.3 copy-start.6
  74.6 2.3 copy-start.41
  76.5 1.2 copy-start.8
  76.5 1.2 copy-start.39
  76.9 1.2 copy-start.9
  76.9 1.2 copy-start.38
  79.6 14.7 %collective-permute-start.4 = (bf16[3,1,10,128]{3,1,2,0:T(2,128)(2,1)S(1)}, bf16[3,1,10,128]{3,1,2,0:T(2,128)(2,1)S(1)}, u32[]{:S(2)}, u32[]{:S(2)}) collective-permute-start(bf16[3,1,10,128]{3,1,2,0:T(2,128)(2,1)S(1)} %get-tuple-element.91), channel_id=1, source_target_pairs={{0,16},{1,17},{2,18},{3,19},{4,20},{5,21},{6,22},{7,23},{8,24},{9,... | collective-permute-start | bytes 23048 | tf_op jit(solution)/shard_map/ppermute | solution.py:16
  84.1 10.1 %collective-permute-start.5 = (bf16[3,1,10,128]{3,1,2,0:T(2,128)(2,1)S(1)}, bf16[3,1,10,128]{3,1,2,0:T(2,128)(2,1)S(1)}, u32[]{:S(2)}, u32[]{:S(2)}) collective-permute-start(bf16[3,1,10,128]{3,1,2,0:T(2,128)(2,1)S(1)} %get-tuple-element.92), channel_id=1, source_target_pairs={{16,0},{17,1},{18,2},{19,3},{20,4},{21,5},{22,6},{23,7},{24,8},{25... | collective-permute-start | bytes 23048 | tf_op jit(solution)/shard_map/ppermute | solution.py:18
  85.5 14.0 %collective-permute-start.8 = (bf16[3,1,10,128]{3,1,2,0:T(2,128)(2,1)S(1)}, bf16[3,1,10,128]{3,1,2,0:T(2,128)(2,1)S(1)}, u32[]{:S(2)}, u32[]{:S(2)}) collective-permute-start(bf16[3,1,10,128]{3,1,2,0:T(2,128)(2,1)S(1)} %get-tuple-element.89), channel_id=1, source_target_pairs={{0,16},{1,17},{2,18},{3,19},{4,20},{5,21},{6,22},{7,23},{8,24},{9,... | collective-permute-start | bytes 23048 | tf_op jit(solution)/shard_map/ppermute | solution.py:16
  90.0 9.5 %collective-permute-start.9 = (bf16[3,1,10,128]{3,1,2,0:T(2,128)(2,1)S(1)}, bf16[3,1,10,128]{3,1,2,0:T(2,128)(2,1)S(1)}, u32[]{:S(2)}, u32[]{:S(2)}) collective-permute-start(bf16[3,1,10,128]{3,1,2,0:T(2,128)(2,1)S(1)} %get-tuple-element.90), channel_id=1, source_target_pairs={{16,0},{17,1},{18,2},{19,3},{20,4},{21,5},{22,6},{23,7},{24,8},{25... | collective-permute-start | bytes 23048 | tf_op jit(solution)/shard_map/ppermute | solution.py:18
  94.3 11.1 %copy-start.27 = (f32[9,384,128]{2,1,0:T(8,128)}, f32[9,384,128]{2,1,0:T(8,128)S(1)}, u32[]{:S(2)}) copy-start(f32[9,384,128]{2,1,0:T(8,128)S(1)} %fusion.9) | copy-start | bytes 5308420
  94.3 11.1 %collective-permute-start.6 = (bf16[3,25,1,128]{3,1,2,0:T(8,128)(2,1)S(1)}, bf16[3,25,1,128]{3,1,2,0:T(8,128)(2,1)S(1)}, u32[]{:S(2)}, u32[]{:S(2)}) collective-permute-start(bf16[3,25,1,128]{3,1,2,0:T(8,128)(2,1)S(1)} %get-tuple-element.85), channel_id=1, source_target_pairs={{0,1},{1,2},{2,3},{3,4},{4,5},{5,6},{6,7},{7,8},{8,9},{9,10},{10,1... | collective-permute-start | bytes 57608 | tf_op jit(solution)/shard_map/ppermute | solution.py:16
  98.2 7.2 %collective-permute-start.7 = (bf16[3,25,1,128]{3,1,2,0:T(8,128)(2,1)S(1)}, bf16[3,25,1,128]{3,1,2,0:T(8,128)(2,1)S(1)}, u32[]{:S(2)}, u32[]{:S(2)}) collective-permute-start(bf16[3,25,1,128]{3,1,2,0:T(8,128)(2,1)S(1)} %get-tuple-element.86), channel_id=1, source_target_pairs={{1,0},{2,1},{3,2},{4,3},{5,4},{6,5},{7,6},{8,7},{9,8},{10,9},{11,1... | collective-permute-start | bytes 57608 | tf_op jit(solution)/shard_map/ppermute | solution.py:18
  99.5 6.5 %copy-start.52 = (bf16[3,1,10,128]{3,1,2,0:T(2,128)(2,1)}, bf16[3,1,10,128]{3,1,2,0:T(2,128)(2,1)S(1)}, u32[]{:S(2)}) copy-start(bf16[3,1,10,128]{3,1,2,0:T(2,128)(2,1)S(1)} %collective-permute-done.9) | copy-start | bytes 23044
  100.2 17.5 %collective-permute-start.10 = (bf16[3,25,1,128]{3,1,2,0:T(8,128)(2,1)}, bf16[3,25,1,128]{3,1,2,0:T(8,128)(2,1)}, u32[]{:S(2)}, u32[]{:S(2)}) collective-permute-start(bf16[3,25,1,128]{3,1,2,0:T(8,128)(2,1)} %get-tuple-element.83), channel_id=1, source_target_pairs={{0,1},{1,2},{2,3},{3,4},{4,5},{5,6},{6,7},{7,8},{8,9},{9,10},{10,1... | collective-permute-start | bytes 57608 | tf_op jit(solution)/shard_map/ppermute | solution.py:16
  104.1 13.6 %collective-permute-start.11 = (bf16[3,25,1,128]{3,1,2,0:T(8,128)(2,1)}, bf16[3,25,1,128]{3,1,2,0:T(8,128)(2,1)}, u32[]{:S(2)}, u32[]{:S(2)}) collective-permute-start(bf16[3,25,1,128]{3,1,2,0:T(8,128)(2,1)} %get-tuple-element.84), channel_id=1, source_target_pairs={{1,0},{2,1},{3,2},{4,3},{5,4},{6,5},{7,6},{8,7},{9,8},{10,9},{11,1... | collective-permute-start | bytes 57608 | tf_op jit(solution)/shard_map/ppermute | solution.py:18
  122.3 1.8 copy-start.28
  124.1 2.5 copy-start.11
  124.1 3.7 %copy-start.12 = (bf16[690,384]{1,0:T(8,128)(2,1)S(1)}, bf16[690,384]{1,0:T(8,128)(2,1)}, u32[]{:S(2)}) copy-start(bf16[690,384]{1,0:T(8,128)(2,1)} %reshape.154) | copy-start | bytes 1589764
  124.1 3.7 %copy-start.37 = (bf16[1,1,3,128,128]{4,3,2,1,0:T(8,128)(2,1)S(1)}, bf16[1,1,3,128,128]{4,3,2,1,0:T(8,128)(2,1)}, u32[]{:S(2)}) copy-start(bf16[1,1,3,128,128]{4,3,2,1,0:T(8,128)(2,1)} %get-tuple-element.41) | copy-start | bytes 294916
  125.1 3.1 %copy-start.13 = (bf16[690,384]{1,0:T(8,128)(2,1)S(1)}, bf16[690,384]{1,0:T(8,128)(2,1)}, u32[]{:S(2)}) copy-start(bf16[690,384]{1,0:T(8,128)(2,1)} %reshape.155) | copy-start | bytes 1589764
  125.2 3.1 %copy-start.36 = (bf16[1,1,3,128,128]{4,3,2,1,0:T(8,128)(2,1)S(1)}, bf16[1,1,3,128,128]{4,3,2,1,0:T(8,128)(2,1)}, u32[]{:S(2)}) copy-start(bf16[1,1,3,128,128]{4,3,2,1,0:T(8,128)(2,1)} %get-tuple-element.40) | copy-start | bytes 294916
  130.9 1.3 copy-start.24
  130.9 1.3 copy-start.35
  131.9 1.7 copy-start.34
  132.1 2.0 copy-start.25
  132.1 2.0 copy-start.33
  132.3 2.1 copy-start.32
  270.0 3.1 %copy-start.26 = (f32[3,3,3,128,128]{4,3,2,1,0:T(8,128)S(1)}, f32[3,3,3,128,128]{4,3,2,1,0:T(8,128)}, u32[]{:S(2)}) copy-start(f32[3,3,3,128,128]{4,3,2,1,0:T(8,128)} %get-tuple-element.7) | copy-start | bytes 5308420
  (23 other events, 25.2 us)
Sparse Core Ops, SparseCore 0:
  124.3 145.6 all-reduce.7
where the time goes:
time: 283 us; the launch traced here: 281 us
  waiting for transfers between devices  90.6 us (32%)
  local copies, waits for them, and re-layouts  62.4 us (22%)
  blocking collectives  45 us (16%)
  starting transfers between devices  31 us (11%)
  matrix products  24.2 us (9%)
  between operations  15.4 us (5%)
  other arithmetic  12.8 us (5%)
    psum x1, waiting for transfers between devices, body(): lax.psum((grad_one, bias_a, grad_two, bias_b), ('ha', 'wa'))  88.1 us
    psum x1, blocking collectives, body(): lax.psum((grad_one, bias_a, grad_two, bias_b), ('ha', 'wa'))  45 us
    reshape x27, local copies, waits for them, and re-layouts, convolve(): wide[step_t:step_t + frames, step_h:step_h + rows].reshape(-1, 3 * inner)  25.2 us
    slice x30, local copies, waits for them, and re-layouts, convolve(): wide[step_t:step_t + frames, step_h:step_h + rows].reshape(-1, 3 * inner)  25.2 us
    ppermute x6, starting transfers between devices, with_halo(): lax.ppermute(tail, axis, [(i, (i + 1) % count) for i in range(ends)])  23.3 us
    dot_general x27, matrix products, convolve(): jnp.dot(slab, kernel[step_t, step_h].reshape(3 * inner, -1), preferred_el...  17.8 us
    ppermute x6, starting transfers between devices, with_halo(): lax.ppermute(head, axis, [((i + 1) % count, i) for i in range(ends)])  7.74 us
    dot_general x18, matrix products, kernel_terms(): lax.dot_general(slab, grads, (((0,), (0,)), ((), ())), preferred_element_...  6.47 us
  transfers between devices with their start and end apart: 13, of which 2 were waited for; matrix products, arithmetic and copies ran while one was open for 12% of the time, Pallas kernels for 0%

commit v1 on v0

--- a/solution.py
+++ b/solution.py
@@ -105,7 +105,7 @@
     grad_one = kernel_terms(first_wide, inner.reshape(-1, chans), frames, rows)
     bias_a = jnp.sum(inner.astype(jnp.float32), axis=(0, 1, 2))
     grad_one, bias_a, grad_two, bias_b = lax.psum(
-        (grad_one, bias_a, grad_two, bias_b), ("ha", "wa")
+        lax.psum((grad_one, bias_a, grad_two, bias_b), "wa"), "ha"
     )
     return (grad_input, grad_one * factor, bias_a * factor, grad_two * factor, bias_b * factor)
 

time: 283 us -> 329 us (1.16)
  waiting for transfers between devices: 90.6 us -> 144 us
  blocking collectives: 45 us -> 34.5 us
  matrix products: 24.2 us -> 29.7 us
  starting transfers between devices: 31 us -> 27.1 us
  local copies, waits for them, and re-layouts: 62.4 us -> 65.9 us
    psum x1 -> x2, waiting for transfers between devices: 88.1 us -> 130 us  [the longest x1 92.5 us: body(): lax.psum((grad_one, bias_a, grad_two, bias_b), 'wa')]
    ppermute x6, waiting for transfers between devices: 2.47 us -> 13.6 us  [with_halo(): lax.ppermute(head, axis, [((i + 1) % count, i) for i in range(ends)])]
    psum x1 -> x2, blocking collectives: 45 us -> 34.5 us  [the longest x1 29.6 us: body(): lax.psum((grad_one, bias_a, grad_two, bias_b), 'wa')]
    dot_general x18, matrix products: 6.47 us -> 12.6 us  [kernel_terms(): lax.dot_general(slab, grads, (((0,), (0,)), ((), ())), preferred_element_...]
    ppermute x6, starting transfers between devices: 23.3 us -> 19.1 us  [with_halo(): lax.ppermute(tail, axis, [(i, (i + 1) % count) for i in range(ends)])]
    slice x30, local copies, waits for them, and re-layouts: 25.2 us -> 29.1 us  [convolve(): wide[step_t:step_t + frames, step_h:step_h + rows].reshape(-1, 3 * inner)]
  transfers between devices with their start and end apart: 13 -> 14, of which waited for: 2 -> 8; matrix products, arithmetic and copies ran while one was open for 12% -> 10% of each run, Pallas kernels for 0% -> 0%
where the time goes in v1:
time: 329 us; the launch traced here: 328 us
  waiting for transfers between devices  144 us (44%)
  local copies, waits for them, and re-layouts  65.9 us (20%)
  blocking collectives  34.5 us (10%)
  matrix products  29.7 us (9%)
  starting transfers between devices  27.1 us (8%)
  between operations  15.3 us (5%)
  other arithmetic  11.3 us (3%)
    psum x1, waiting for transfers between devices, body(): lax.psum((grad_one, bias_a, grad_two, bias_b), 'wa')  92.5 us
    psum x1, waiting for transfers between devices, body(): lax.psum(lax.psum((grad_one, bias_a, grad_two, bias_b), 'wa'), 'ha')  37.6 us
    psum x1, blocking collectives, body(): lax.psum((grad_one, bias_a, grad_two, bias_b), 'wa')  29.6 us
    slice x30, local copies, waits for them, and re-layouts, convolve(): wide[step_t:step_t + frames, step_h:step_h + rows].reshape(-1, 3 * inner)  29.1 us
    reshape x27, local copies, waits for them, and re-layouts, convolve(): wide[step_t:step_t + frames, step_h:step_h + rows].reshape(-1, 3 * inner)  26 us
    ppermute x6, starting transfers between devices, with_halo(): lax.ppermute(tail, axis, [(i, (i + 1) % count) for i in range(ends)])  19.1 us
    dot_general x27, matrix products, convolve(): jnp.dot(slab, kernel[step_t, step_h].reshape(3 * inner, -1), preferred_el...  17.1 us
    ppermute x6, waiting for transfers between devices, with_halo(): lax.ppermute(head, axis, [((i + 1) % count, i) for i in range(ends)])  13.6 us
  transfers between devices with their start and end apart: 14, of which 8 were waited for; matrix products, arithmetic and copies ran while one was open for 10% of the time, Pallas kernels for 0%

profile of v1, /device:TPU:0, one launch (start us, length us, event | category | flops | bytes accessed | tf_op | source)
XLA Modules:
  0.0 327.5 jit_solution(12337049045566607485)
XLA Ops:
  9.2 4.9 %collective-permute-start = (bf16[2,3,1,10,128]{4,2,3,1,0:T(2,128)(2,1)S(1)}, bf16[2,3,1,10,128]{4,2,3,1,0:T(2,128)(2,1)S(1)}, u32[]{:S(2)}, u32[]{:S(2)}) collective-permute-start(bf16[2,3,1,10,128]{4,2,3,1,0:T(2,128)(2,1)S(1)} %get-tuple-element.79), channel_id=1, source_target_pairs={{0,16},{1,17},{2,18},{3,19},{4,20},{5,21},{6,22},{7,23},{8,24},{9,... | collective-permute-start | bytes 46088 | tf_op jit(solution)/shard_map/ppermute | solution.py:16
  14.1 1.3 collective-permute-start.1
  15.4 2.0 copy.18
  18.5 1.4 collective-permute-done.1
  19.9 1.3 collective-permute-start.2
  21.2 1.3 collective-permute-start.3
  23.5 2.6 collective-permute-done.3
  26.4 1.3 pad_slice_fusion.2
  27.9 2.2 fusion.63
  31.3 1.2 copy.19
  33.4 1.2 copy.20
  35.6 1.2 copy.21
  37.8 1.2 copy.22
  40.0 1.2 copy.23
  44.4 1.3 pad_maximum_fusion.1
  45.7 2.5 fusion.62
  49.3 1.2 copy.28
  51.5 1.2 copy.29
  53.6 1.2 copy.30
  66.6 1.2 copy.26
  68.9 1.5 fusion.72
  70.4 1.4 convolution_add_fusion.15
  76.3 1.3 fusion.71
  77.7 1.6 convolution_add_fusion.23
  84.2 3.1 collective-permute-start.8
  87.4 1.3 collective-permute-start.9
  91.6 1.4 collective-permute-done.9
  93.0 3.3 collective-permute-start.10
  96.3 1.3 collective-permute-start.11
  98.0 2.3 collective-permute-done.11
  110.2 1.4 copy.39
  111.7 3.2 collective-permute-start.4
  114.8 1.3 collective-permute-start.5
  116.3 4.2 %collective-permute-done.5 = bf16[3,1,10,128]{3,1,2,0:T(2,128)(2,1)S(1)} collective-permute-done((bf16[3,1,10,128]{3,1,2,0:T(2,128)(2,1)S(1)}, bf16[3,1,10,128]{3,1,2,0:T(2,128)(2,1)S(1)}, u32[]{:S(2)}, u32[]{:S(2)}) %collective-permute-start.5) | collective-permute-done | bytes 7712 | tf_op jit(solution)/shard_map/ppermute | solution.py:18
  120.5 3.3 %collective-permute-start.6 = (bf16[3,25,1,128]{3,1,2,0:T(8,128)(2,1)S(1)}, bf16[3,25,1,128]{3,1,2,0:T(8,128)(2,1)S(1)}, u32[]{:S(2)}, u32[]{:S(2)}) collective-permute-start(bf16[3,25,1,128]{3,1,2,0:T(8,128)(2,1)S(1)} %get-tuple-element.89), channel_id=1, source_target_pairs={{0,1},{1,2},{2,3},{3,4},{4,5},{5,6},{6,7},{7,8},{8,9},{9,10},{10,1... | collective-permute-start | bytes 57608 | tf_op jit(solution)/shard_map/ppermute | solution.py:16
  123.8 1.5 collective-permute-start.7
  126.2 1.7 collective-permute-done.7
  128.0 92.5 %all-reduce.11.cloned.1.call-done = (f32[3,3,3,128,128]{4,3,2,1,0:T(8,128)}, f32[3,3,3,128,128]{4,3,2,1,0:T(8,128)}) async-done(((f32[3,3,3,128,128]{4,3,2,1,0:T(8,128)}, f32[3,3,3,128,128]{4,3,2,1,0:T(8,128)}), (f32[3,3,3,128,128]{4,3,2,1,0:T(8,128)}, f32[3,3,3,128,128]{4,3,2,1,0:T(8,128)})) %all-reduce.11.cloned.1.call-update) | async-done | bytes 3538960 | tf_op jit(solution)/shard_map/psum | solution.py:108
  221.0 1.9 fusion.61
  226.2 1.3 copy.41
  228.5 1.2 copy.42
  236.6 1.3 fusion.73
  237.9 1.3 convolution_add_fusion.7
  243.1 29.6 %all-reduce.4 = (f32[128]{0:T(128)S(1)}, f32[128]{0:T(128)S(1)}) all-reduce(f32[128]{0:T(128)S(1)} %get-tuple-element.97, f32[128]{0:T(128)S(1)} %get-tuple-element.91), channel_id=1, replica_groups=mesh['ha'=2,'wa'=16] {'wa'}, use_global_device_ids=true, to_apply=%region_3.4 | all-reduce | flops 256 | bytes 2048 | tf_op jit(solution)/shard_map/psum | solution.py:108
  272.7 4.9 %all-reduce.6 = (f32[128]{0:T(128)S(1)}, f32[128]{0:T(128)S(1)}) all-reduce(f32[128]{0:T(128)S(1)} %get-tuple-element.5, f32[128]{0:T(128)S(1)} %get-tuple-element.6), channel_id=1, replica_groups=mesh['ha'=2,'wa'=16] {'ha'}, use_global_device_ids=true, to_apply=%region_4.5 | all-reduce | flops 256 | bytes 2048 | tf_op jit(solution)/shard_map/psum | solution.py:107
  278.7 37.6 %all-reduce.13.cloned.1.call-done = (f32[3,3,3,128,128]{4,3,2,1,0:T(8,128)}, f32[3,3,3,128,128]{4,3,2,1,0:T(8,128)}) async-done(((f32[3,3,3,128,128]{4,3,2,1,0:T(8,128)}, f32[3,3,3,128,128]{4,3,2,1,0:T(8,128)}), (f32[3,3,3,128,128]{4,3,2,1,0:T(8,128)}, f32[3,3,3,128,128]{4,3,2,1,0:T(8,128)})) %all-reduce.13.cloned.1.call-update) | async-done | bytes 3538960 | tf_op jit(solution)/shard_map/psum | solution.py:107
  316.2 3.1 broadcast_multiply_fusion
  319.3 1.4 broadcast_multiply_fusion.1
  (234 shorter events, 68.3 us)
Async XLA Ops:
  7.2 213.4 %all-reduce.11.cloned.1.call-start = ((), (), s32[]{:S(2)}) async-start(), calls=%async_computation | async-start | bytes 7077888 | tf_op jit(solution)/shard_map/psum | solution.py:108
  9.2 9.3 %collective-permute-start = (bf16[2,3,1,10,128]{4,2,3,1,0:T(2,128)(2,1)S(1)}, bf16[2,3,1,10,128]{4,2,3,1,0:T(2,128)(2,1)S(1)}, u32[]{:S(2)}, u32[]{:S(2)}) collective-permute-start(bf16[2,3,1,10,128]{4,2,3,1,0:T(2,128)(2,1)S(1)} %get-tuple-element.79), channel_id=1, source_target_pairs={{0,16},{1,17},{2,18},{3,19},{4,20},{5,21},{6,22},{7,23},{8,24},{9,... | collective-permute-start | bytes 46088 | tf_op jit(solution)/shard_map/ppermute | solution.py:16
  14.1 5.8 %collective-permute-start.1 = (bf16[2,3,1,10,128]{4,2,3,1,0:T(2,128)(2,1)S(1)}, bf16[2,3,1,10,128]{4,2,3,1,0:T(2,128)(2,1)S(1)}, u32[]{:S(2)}, u32[]{:S(2)}) collective-permute-start(bf16[2,3,1,10,128]{4,2,3,1,0:T(2,128)(2,1)S(1)} %get-tuple-element.80), channel_id=1, source_target_pairs={{16,0},{17,1},{18,2},{19,3},{20,4},{21,5},{22,6},{23,7},{24,8},{25... | collective-permute-start | bytes 46088 | tf_op jit(solution)/shard_map/ppermute | solution.py:18
  17.4 2.5 copy-start.1
  17.4 5.1 %copy-start = (bf16[3,3,3,128,128]{4,3,2,1,0:T(8,128)(2,1)S(1)}, bf16[3,3,3,128,128]{4,3,2,1,0:T(8,128)(2,1)}, u32[]{:S(2)}) copy-start(bf16[3,3,3,128,128]{4,3,2,1,0:T(8,128)(2,1)} %param.11) | copy-start | bytes 2654212
  19.9 3.5 %collective-permute-start.2 = (bf16[2,3,25,1,128]{4,2,3,1,0:T(8,128)(2,1)S(1)}, bf16[2,3,25,1,128]{4,2,3,1,0:T(8,128)(2,1)S(1)}, u32[]{:S(2)}, u32[]{:S(2)}) collective-permute-start(bf16[2,3,25,1,128]{4,2,3,1,0:T(8,128)(2,1)S(1)} %get-tuple-element.77), channel_id=1, source_target_pairs={{0,1},{1,2},{2,3},{3,4},{4,5},{5,6},{6,7},{7,8},{8,9},{9,10},{10,1... | collective-permute-start | bytes 115208 | tf_op jit(solution)/shard_map/ppermute | solution.py:16
  21.2 4.8 %collective-permute-start.3 = (bf16[2,3,25,1,128]{4,2,3,1,0:T(8,128)(2,1)S(1)}, bf16[2,3,25,1,128]{4,2,3,1,0:T(8,128)(2,1)S(1)}, u32[]{:S(2)}, u32[]{:S(2)}) collective-permute-start(bf16[2,3,25,1,128]{4,2,3,1,0:T(8,128)(2,1)S(1)} %get-tuple-element.78), channel_id=1, source_target_pairs={{1,0},{2,1},{3,2},{4,3},{5,4},{6,5},{7,6},{8,7},{9,8},{10,9},{11,1... | collective-permute-start | bytes 115208 | tf_op jit(solution)/shard_map/ppermute | solution.py:18
  65.6 3.2 copy-start.45
  66.6 3.7 %copy-start.44 = (bf16[1,1,3,128,128]{4,3,2,1,0:T(8,128)(2,1)S(1)}, bf16[1,1,3,128,128]{4,3,2,1,0:T(8,128)(2,1)}, u32[]{:S(2)}) copy-start(bf16[1,1,3,128,128]{4,3,2,1,0:T(8,128)(2,1)} %get-tuple-element.56) | copy-start | bytes 294916
  67.8 4.0 %copy-start.43 = (bf16[1,1,3,128,128]{4,3,2,1,0:T(8,128)(2,1)S(1)}, bf16[1,1,3,128,128]{4,3,2,1,0:T(8,128)(2,1)}, u32[]{:S(2)}) copy-start(bf16[1,1,3,128,128]{4,3,2,1,0:T(8,128)(2,1)} %get-tuple-element.55) | copy-start | bytes 294916
  68.9 3.0 copy-start.9
  68.9 3.4 %copy-start.10 = (bf16[690,384]{1,0:T(8,128)(2,1)S(1)}, bf16[690,384]{1,0:T(8,128)(2,1)}, u32[]{:S(2)}) copy-start(bf16[690,384]{1,0:T(8,128)(2,1)} %reshape.144) | copy-start | bytes 1589764
  68.9 3.4 %copy-start.42 = (bf16[1,1,3,128,128]{4,3,2,1,0:T(8,128)(2,1)S(1)}, bf16[1,1,3,128,128]{4,3,2,1,0:T(8,128)(2,1)}, u32[]{:S(2)}) copy-start(bf16[1,1,3,128,128]{4,3,2,1,0:T(8,128)(2,1)} %get-tuple-element.54) | copy-start | bytes 294916
  70.4 2.2 copy-start.11
  70.4 2.2 copy-start.41
  73.8 2.5 copy-start.2
  75.2 4.1 %copy-start.36 = (bf16[1,1,3,128,128]{4,3,2,1,0:T(8,128)(2,1)S(1)}, bf16[1,1,3,128,128]{4,3,2,1,0:T(8,128)(2,1)}, u32[]{:S(2)}) copy-start(bf16[1,1,3,128,128]{4,3,2,1,0:T(8,128)(2,1)} %get-tuple-element.64) | copy-start | bytes 294916
  76.3 3.0 copy-start.3
  76.3 3.4 %copy-start.4 = (bf16[690,384]{1,0:T(8,128)(2,1)S(1)}, bf16[690,384]{1,0:T(8,128)(2,1)}, u32[]{:S(2)}) copy-start(bf16[690,384]{1,0:T(8,128)(2,1)} %reshape.134) | copy-start | bytes 1589764
  76.3 3.4 %copy-start.35 = (bf16[1,1,3,128,128]{4,3,2,1,0:T(8,128)(2,1)S(1)}, bf16[1,1,3,128,128]{4,3,2,1,0:T(8,128)(2,1)}, u32[]{:S(2)}) copy-start(bf16[1,1,3,128,128]{4,3,2,1,0:T(8,128)(2,1)} %get-tuple-element.63) | copy-start | bytes 294916
  77.7 2.4 copy-start.5
  77.7 2.4 copy-start.34
  80.5 1.2 copy-start.30
  80.5 1.2 copy-start.51
  80.5 1.2 copy-start.54
  80.5 1.2 copy-start.55
  80.5 1.2 copy-start.56
  84.2 13.4 %copy-start.24 = (bf16[3,23,10,128]{3,1,2,0:T(8,128)(2,1)}, bf16[3,23,10,128]{3,1,2,0:T(8,128)(2,1)S(1)}, u32[]{:S(2)}) copy-start(bf16[3,23,10,128]{3,1,2,0:T(8,128)(2,1)S(1)} %get-tuple-element.70) | copy-start | bytes 529924
  84.2 7.4 %collective-permute-start.8 = (bf16[3,1,10,128]{3,1,2,0:T(2,128)(2,1)S(1)}, bf16[3,1,10,128]{3,1,2,0:T(2,128)(2,1)S(1)}, u32[]{:S(2)}, u32[]{:S(2)}) collective-permute-start(bf16[3,1,10,128]{3,1,2,0:T(2,128)(2,1)S(1)} %get-tuple-element.93), channel_id=1, source_target_pairs={{0,16},{1,17},{2,18},{3,19},{4,20},{5,21},{6,22},{7,23},{8,24},{9,... | collective-permute-start | bytes 23048 | tf_op jit(solution)/shard_map/ppermute | solution.py:16
  87.4 5.6 %collective-permute-start.9 = (bf16[3,1,10,128]{3,1,2,0:T(2,128)(2,1)S(1)}, bf16[3,1,10,128]{3,1,2,0:T(2,128)(2,1)S(1)}, u32[]{:S(2)}, u32[]{:S(2)}) collective-permute-start(bf16[3,1,10,128]{3,1,2,0:T(2,128)(2,1)S(1)} %get-tuple-element.94), channel_id=1, source_target_pairs={{16,0},{17,1},{18,2},{19,3},{20,4},{21,5},{22,6},{23,7},{24,8},{25... | collective-permute-start | bytes 23048 | tf_op jit(solution)/shard_map/ppermute | solution.py:18
  93.0 5.0 %collective-permute-start.10 = (bf16[3,25,1,128]{3,1,2,0:T(8,128)(2,1)S(1)}, bf16[3,25,1,128]{3,1,2,0:T(8,128)(2,1)S(1)}, u32[]{:S(2)}, u32[]{:S(2)}) collective-permute-start(bf16[3,25,1,128]{3,1,2,0:T(8,128)(2,1)S(1)} %get-tuple-element.87), channel_id=1, source_target_pairs={{0,1},{1,2},{2,3},{3,4},{4,5},{5,6},{6,7},{7,8},{8,9},{9,10},{10,1... | collective-permute-start | bytes 57608 | tf_op jit(solution)/shard_map/ppermute | solution.py:16
  96.3 4.0 %collective-permute-start.11 = (bf16[3,25,1,128]{3,1,2,0:T(8,128)(2,1)S(1)}, bf16[3,25,1,128]{3,1,2,0:T(8,128)(2,1)S(1)}, u32[]{:S(2)}, u32[]{:S(2)}) collective-permute-start(bf16[3,25,1,128]{3,1,2,0:T(8,128)(2,1)S(1)} %get-tuple-element.88), channel_id=1, source_target_pairs={{1,0},{2,1},{3,2},{4,3},{5,4},{6,5},{7,6},{8,7},{9,8},{10,9},{11,1... | collective-permute-start | bytes 57608 | tf_op jit(solution)/shard_map/ppermute | solution.py:18
  97.9 2.9 copy-start.27
  110.2 1.5 copy-start.25
  110.2 206.0 %all-reduce.13.cloned.1.call-start = ((), (), s32[]{:S(2)}) async-start(), calls=%async_computation.1 | async-start | bytes 7077888 | tf_op jit(solution)/shard_map/psum | solution.py:107
  111.7 4.6 %collective-permute-start.4 = (bf16[3,1,10,128]{3,1,2,0:T(2,128)(2,1)S(1)}, bf16[3,1,10,128]{3,1,2,0:T(2,128)(2,1)S(1)}, u32[]{:S(2)}, u32[]{:S(2)}) collective-permute-start(bf16[3,1,10,128]{3,1,2,0:T(2,128)(2,1)S(1)} %get-tuple-element.95), channel_id=1, source_target_pairs={{0,16},{1,17},{2,18},{3,19},{4,20},{5,21},{6,22},{7,23},{8,24},{9,... | collective-permute-start | bytes 23048 | tf_op jit(solution)/shard_map/ppermute | solution.py:16
  114.8 5.6 %collective-permute-start.5 = (bf16[3,1,10,128]{3,1,2,0:T(2,128)(2,1)S(1)}, bf16[3,1,10,128]{3,1,2,0:T(2,128)(2,1)S(1)}, u32[]{:S(2)}, u32[]{:S(2)}) collective-permute-start(bf16[3,1,10,128]{3,1,2,0:T(2,128)(2,1)S(1)} %get-tuple-element.96), channel_id=1, source_target_pairs={{16,0},{17,1},{18,2},{19,3},{20,4},{21,5},{22,6},{23,7},{24,8},{25... | collective-permute-start | bytes 23048 | tf_op jit(solution)/shard_map/ppermute | solution.py:18
  120.5 5.7 %collective-permute-start.6 = (bf16[3,25,1,128]{3,1,2,0:T(8,128)(2,1)S(1)}, bf16[3,25,1,128]{3,1,2,0:T(8,128)(2,1)S(1)}, u32[]{:S(2)}, u32[]{:S(2)}) collective-permute-start(bf16[3,25,1,128]{3,1,2,0:T(8,128)(2,1)S(1)} %get-tuple-element.89), channel_id=1, source_target_pairs={{0,1},{1,2},{2,3},{3,4},{4,5},{5,6},{6,7},{7,8},{8,9},{9,10},{10,1... | collective-permute-start | bytes 57608 | tf_op jit(solution)/shard_map/ppermute | solution.py:16
  123.8 4.0 %collective-permute-start.7 = (bf16[3,25,1,128]{3,1,2,0:T(8,128)(2,1)S(1)}, bf16[3,25,1,128]{3,1,2,0:T(8,128)(2,1)S(1)}, u32[]{:S(2)}, u32[]{:S(2)}) collective-permute-start(bf16[3,25,1,128]{3,1,2,0:T(8,128)(2,1)S(1)} %get-tuple-element.90), channel_id=1, source_target_pairs={{1,0},{2,1},{3,2},{4,3},{5,4},{6,5},{7,6},{8,7},{9,8},{10,9},{11,1... | collective-permute-start | bytes 57608 | tf_op jit(solution)/shard_map/ppermute | solution.py:18
  234.4 2.2 copy-start.16
  235.5 2.4 copy-start.17
  235.6 3.6 %copy-start.18 = (bf16[690,384]{1,0:T(8,128)(2,1)S(1)}, bf16[690,384]{1,0:T(8,128)(2,1)}, u32[]{:S(2)}) copy-start(bf16[690,384]{1,0:T(8,128)(2,1)} %reshape.153) | copy-start | bytes 1589764
  236.6 2.7 copy-start.50
  236.6 3.0 copy-start.19
  236.6 3.0 copy-start.49
  237.9 2.1 copy-start.20
  237.9 2.1 copy-start.48
  316.2 3.1 copy-start.26
  (23 other events, 25.8 us)
Sparse Core Ops, SparseCore 0:
  110.3 110.1 all-reduce.10
  222.9 93.2 all-reduce.12
